TPU v7x, 32 devices: a whole 2x2x4 slice. The times are simulated.
32 devices in a mesh: band: 8 (over y, x, core), space: 4 (over z).
Axes of the slice: x: 2, y: 2, z: 4, core: 2. Of those that a mesh axis runs over, the one named last changes fastest.
Arguments:
- orbitals: bfloat16 [8, 192, 192, 192], P('band', 'space'), may hold values from -4 to 4
- occupations: float32 [8], P('band'), may hold values from 0.25 to 1
- shifts: float32 [8], P('band'), may hold values from 0.25 to 2
- perturbations: float32 [1, 192, 192, 192], P(None, 'space'), may hold values from -3 to 3
- local_potential: float32 [192, 192, 192], P('space'), may hold values from 0 to 1
Outputs:
- response_potential: float32 [1, 192, 192, 192], P(None, 'space', 'band')
All inputs are finite; a program needn't handle non-finite values.
Results may differ from a plain program's by a relative error of at most 0.0003.
Values sent between devices are 32-bit elements; how exact they have to be, the bound alone decides.
No kernel may reach another device: no remote copies, remote signals or barrier semaphores. Data moves between devices by JAX's collectives and lax.ppermute only.
A program may use at most 320 MiB of HBM per device.

v0:
```python
import math

import jax
import jax.numpy as jnp
import numpy as np
from jax import lax
from jax.experimental import pallas as pl
from jax.experimental.pallas import tpu as pltpu
from jax.sharding import PartitionSpec as P


LANES = 128
REACH = 4
COEFFS = (-205.0 / 72.0, 8.0 / 5.0, -1.0 / 5.0, 8.0 / 315.0, -1.0 / 560.0)
DENOM = 5040.0
MIB = 1 << 20
UNROLL = 4
F32 = jnp.float32
BF16 = jnp.bfloat16


def cas_np(rows, cols, count):
    prod = (np.asarray(rows, np.int64)[:, None] * np.asarray(cols, np.int64)[None, :]) % count
    ang = prod * (2.0 * math.pi / count)
    return (np.cos(ang) + np.sin(ang)).astype(np.float32)


def split_np(table):
    hi = table.astype(BF16)
    lo = (table - hi.astype(np.float32)).astype(BF16)
    return hi, lo


def circulant_np(count):
    mat = np.zeros((count, count), np.float64)
    for m in range(1, REACH + 1):
        for i in range(count):
            mat[i, (i + m) % count] += COEFFS[m] * DENOM
            mat[i, (i - m) % count] += COEFFS[m] * DENOM
    return np.round(mat).astype(np.float32).astype(BF16)


def partner(b, stage, bits):
    if stage == 0:
        return b ^ 1
    bit = stage if b % 2 == 0 else bits - stage
    return b ^ (1 << bit)


def block_orders(n_band):
    bits = n_band.bit_length() - 1
    held = {b: [b] for b in range(n_band)}
    for stage in range(bits - 1, -1, -1):
        held = {b: held[partner(b, stage, bits)] + held[b] for b in range(n_band)}
    return np.array([held[b] for b in range(n_band)], np.int32)


def split(values):
    hi = values.astype(BF16)
    lo = (values - hi.astype(F32)).astype(BF16)
    return hi, lo


def mm(a, b):
    return jnp.dot(a, b, preferred_element_type=F32)


def mm_nt(a, b):
    return lax.dot_general(a, b, (((1,), (1,)), ((), ())), preferred_element_type=F32)


def mm3(ah, al, b):
    bh, bl = split(b)
    return mm(ah, bh) + mm(ah, bl) + mm(al, bh)


def mm3_right(a, bh, bl):
    ah, al = split(a)
    return mm(ah, bh) + mm(al, bh) + mm(ah, bl)


def lap_yz(field, ccy_ref, cc_ref):
    hi, lo = split(field)
    stack = jnp.concatenate([hi, lo], axis=0)
    return mm(ccy_ref[...], stack) + mm(hi, cc_ref[...]) + mm(lo, cc_ref[...])


def spectra(pairs, before, begin, finish, ty_ref, tz_ref, ccy_ref, cc_ref, outs, lap, part, stack, freq):
    n = tz_ref.shape[0]
    half = n // 2
    wide = 2 * LANES
    for k in range(3):
        freq[:, :, k * wide + n:(k + 1) * wide] = jnp.zeros((UNROLL, n, wide - n), BF16)

    def sums(plane, slot):
        field, total = begin(plane, slice(0, n))
        hi, lo = split(field)
        lap[slot, :n, :] = hi
        lap[slot, n:, :] = lo
        part[slot] = total

    def stencil(slot):
        return mm(ccy_ref[...], lap[slot]) + mm(lap[slot, :n, :], cc_ref[...]) + mm(lap[slot, n:, :], cc_ref[...])

    def keep_rho(plane, slot, grad):
        rh, rl = split(finish(plane, part[slot], grad))
        for k, cells in enumerate((rh, rl, rh)):
            stack[slot, k * n:(k + 1) * n, :] = cells

    def keep_y(slot, values):
        eh, el = split(values)
        for k, cells in enumerate((eh, el, eh)):
            freq[slot, :, k * wide:k * wide + n] = cells

    def give(pair, odd, spec):
        cut = odd * (LANES // 2)
        for o, ref in enumerate(outs):
            cells = spec[o * half:(o + 1) * half]
            ref[pair, odd] = cells[:, :LANES]
            ref[pair, 2, :, cut:cut + LANES // 2] = cells[:, LANES:]

    def step(t, carry):
        before(t)
        for j in range(UNROLL):
            sums(UNROLL * t + j, j)
        grads = [stencil(j) for j in range(UNROLL)]
        for j in range(UNROLL):
            keep_rho(UNROLL * t + j, j, grads[j])
        for j in range(UNROLL):
            keep_y(j, mm(ty_ref[...], stack[j]))
        for j in range(UNROLL):
            give(UNROLL // 2 * t + j // 2, j % 2, mm_nt(tz_ref[...], freq[j]))
        return carry

    lax.fori_loop(0, 2 * pairs // UNROLL, step, 0)


def pack_plane(plane):
    n = plane.shape[0]
    tail = jnp.concatenate([plane[: n // 2, LANES:], plane[n // 2:, LANES:]], axis=1)
    return plane[:, :LANES], tail


def edges_kernel(share_ref, orb_hbm, pert_hbm, low, high, orb, pert, packed, sem):
    count_x, n = orb_hbm.shape[0], orb_hbm.shape[1]
    per_plane = n + n // 2
    whole = REACH * per_plane
    rows = whole // 2
    copies = []
    for side, start in enumerate((0, count_x - REACH)):
        for k, (src, dst) in enumerate(((orb_hbm, orb), (pert_hbm, pert))):
            c = pltpu.make_async_copy(src.at[pl.ds(start, REACH)], dst.at[side], sem.at[side, k])
            c.start()
            copies.append(c)
    for c in copies:
        c.wait()
    mine = pl.multiple_of(lax.rem(lax.axis_index("band"), 2) * rows, 8)
    for side, out in enumerate((low, high)):
        for j in range(REACH):
            main, tail = pack_plane(orb[side, j].astype(F32))
            out[pl.ds(j * per_plane, n), :] = main
            out[pl.ds(j * per_plane + n, n // 2), :] = tail
            main, tail = pack_plane(pert[side, j])
            packed[pl.ds(j * per_plane, n), :] = main
            packed[pl.ds(j * per_plane + n, n // 2), :] = tail
        out[pl.ds(whole, rows), :] = packed[pl.ds(mine, rows), :]


def order_rows(n_band, share_ref, base_ref, part, tz):
    width, n = base_ref.shape[1:]
    wide = 2 * LANES
    for p in range(n_band):
        part[0, p * width:(p + 1) * width, :] = base_ref[share_ref[lax.axis_index("band"), p]]
    hi, lo = split(part[0])
    for k, cells in enumerate((hi, hi, lo)):
        tz[:, k * wide:k * wide + n] = cells
        tz[:, k * wide + n:(k + 1) * wide] = jnp.zeros((n, wide - n), BF16)


C_SRC, C_A, C_B, C_S, C_D0, C_G, C_P, C_T = 0, 1, 2, 3, 8, 9, 10, 11


def first_apply(co, d0, idx, pot, ccy_ref, cc_ref):
    centre = d0[idx]
    total = (co[C_A] - co[C_B] * pot) * centre + co[C_S] * lap_yz(centre, ccy_ref, cc_ref)
    for m in range(1, REACH + 1):
        total = total + (co[C_S] * (COEFFS[m] * DENOM)) * (d0[idx + m] + d0[idx - m])
    return total


def second_begin(co, d0, d1, idx, at, pot):
    centre = d1[idx, at]
    total = co[C_D0] * d0 + (co[C_G] - co[C_P] * pot) * centre
    for m in range(1, REACH + 1):
        total = total + (co[C_T] * (COEFFS[m] * DENOM)) * (d1[idx + m, at] + d1[idx - m, at])
    return centre, total


def first_kernel(n_band, share_ref, co, orb_hbm, pert_hbm, pot_hbm, cc_ref, ccy_ref, ty_ref, base_ref,
                 d1_hbm, send_ref, keep_ref, orb, d0, pot, d1, tz, lap, part, stack, freq, sem, out_sem):
    count_x = orb.shape[0]
    groups = count_x // REACH
    arrays = ((orb_hbm, orb), (pert_hbm, d0), (pot_hbm, pot))

    def copy(k, g):
        src, dst = arrays[k]
        where = pl.ds(g * REACH, REACH)
        return pltpu.make_async_copy(src.at[where], dst.at[where], sem.at[k, g])

    def copy_out(g):
        where = pl.ds(g * REACH, REACH)
        return pltpu.make_async_copy(d1.at[where], d1_hbm.at[where], out_sem.at[g])

    def source(g):
        for k in range(3):
            copy(k, g).wait()
        for j in range(REACH):
            x = g * REACH + j
            d0[x] = co[C_SRC] * (d0[x] * orb[x].astype(F32))

    for g in range(groups):
        for k in range(3):
            copy(k, g).start()
    order_rows(n_band, share_ref, base_ref, part, tz)
    source(0)
    source(1)

    def step(g, carry):
        source(g)
        for j in range(REACH):
            x = (g - 1) * REACH + j
            d1[x] = first_apply(co, d0, x, pot[x], ccy_ref, cc_ref)
        copy_out(g - 1).start()
        return carry

    lax.fori_loop(2, groups, step, 0)
    lead = 2 * REACH

    def begin(p, at):
        return second_begin(co, d0[lead + p, at], d1, lead + p, at, pot[lead + p, at])

    def finish(p, total, grad):
        return orb[lead + p].astype(F32) * (total + co[C_T] * grad)

    spectra(send_ref.shape[0], lambda t: None, begin, finish, ty_ref, tz, ccy_ref, cc_ref, (send_ref, keep_ref),
            lap, part, stack, freq)

    def done(g, carry):
        copy_out(g).wait()
        return carry

    lax.fori_loop(1, groups - 1, done, 0)


def inner_kernel(n_band, start, share_ref, co, orb_hbm, pert_hbm, pot_hbm, d1_hbm, cc_ref, ccy_ref, ty_ref, base_ref,
                 send_ref, keep_ref, orb, pert, pot, d1, tz, lap, part, stack, freq, sem, first_sem):
    pairs = send_ref.shape[0]
    lead = 2 * REACH
    arrays = (
        (orb_hbm, orb, start, 0), (pert_hbm, pert, start, 0), (pot_hbm, pot, start, 0),
        (d1_hbm, d1, start + REACH, lead),
    )

    def copy(k, i):
        src, dst, at, to = arrays[k]
        return pltpu.make_async_copy(src.at[pl.ds(at + 2 * i, 2)], dst.at[pl.ds(to + 2 * i, 2)], sem.at[k, i])

    ahead = pltpu.make_async_copy(d1_hbm.at[pl.ds(start - REACH, lead)], d1.at[pl.ds(0, lead)], first_sem.at[0])
    ahead.start()
    for i in range(pairs):
        for k in range(4):
            copy(k, i).start()
    order_rows(n_band, share_ref, base_ref, part, tz)
    ahead.wait()

    def before(t):
        for i in range(UNROLL // 2):
            for k in range(4):
                copy(k, UNROLL // 2 * t + i).wait()

    def begin(p, at):
        d0 = co[C_SRC] * (pert[p, at] * orb[p, at].astype(F32))
        return second_begin(co, d0, d1, p + REACH, at, pot[p, at])

    def finish(p, total, grad):
        return orb[p].astype(F32) * (total + co[C_T] * grad)

    spectra(pairs, before, begin, finish, ty_ref, tz, ccy_ref, cc_ref, (send_ref, keep_ref), lap, part, stack, freq)


def boundary_kernel(n_band, side, share_ref, co, orb_hbm, pert_hbm, pot_hbm, d1_hbm, mine, other,
                    cc_ref, ccy_ref, ty_ref, base_ref, send_ref, keep_ref,
                    orb, psi, pert, pot, d0, d1, packed, tz, lap, part, stack, freq, sem):
    count_x, n = orb_hbm.shape[0], orb_hbm.shape[1]
    per_plane = n + n // 2
    whole = REACH * per_plane
    span = 3 * REACH
    own = (0, count_x - 2 * REACH)[side]
    at_own = (REACH, 0)[side]
    halo = (0, 2 * REACH)[side]
    d1_own = (REACH, count_x - 3 * REACH)[side]
    d1_at = (3 * REACH, 0)[side]
    far = (0, 3 * REACH)[side]
    copies = [
        pltpu.make_async_copy(src.at[pl.ds(own, 2 * REACH)], dst.at[pl.ds(at_own, 2 * REACH)], sem.at[k])
        for k, (src, dst) in enumerate(((orb_hbm, orb), (pert_hbm, pert), (pot_hbm, pot)))
    ]
    copies.append(pltpu.make_async_copy(
        d1_hbm.at[pl.ds(d1_own, 2 * REACH)], d1.at[pl.ds(d1_at, 2 * REACH)], sem.at[3]))
    for c in copies:
        c.start()
    order_rows(n_band, share_ref, base_ref, part, tz)
    zero = jnp.zeros((n, n), F32)
    core = lax.rem(lax.axis_index("band"), 2)
    rows = whole // 2
    packed[pl.ds(pl.multiple_of(core * rows, 8), rows), :] = mine[pl.ds(whole, rows), :]
    packed[pl.ds(pl.multiple_of((1 - core) * rows, 8), rows), :] = other[...]
    for j in range(REACH):
        for src, dst in ((mine, psi), (packed, d0)):
            base = j * per_plane
            tail = src[pl.ds(base + n, n // 2), :]
            dst[halo + j, :, :LANES] = src[pl.ds(base, n), :]
            dst[halo + j, : n // 2, LANES:] = tail[:, : n - LANES]
            dst[halo + j, n // 2:, LANES:] = tail[:, n - LANES:]
        pot[halo + j] = zero
        d0[halo + j] = co[C_SRC] * (d0[halo + j] * psi[halo + j])
    for j in range(2 * REACH):
        d1[far + j] = zero
    for c in copies:
        c.wait()

    def fill(i, carry):
        wave = orb[at_own + i].astype(F32)
        psi[at_own + i] = wave
        d0[at_own + i] = co[C_SRC] * (pert[at_own + i] * wave)
        return carry

    lax.fori_loop(0, 2 * REACH, fill, 0)
    for j in range(REACH):
        d1[2 * REACH + j] = first_apply(co, d0, REACH + j, pot[REACH + j], ccy_ref, cc_ref)
    for j in range(REACH):
        d0[halo + j] = zero

    def begin(p, at):
        return second_begin(co, d0[p, at], d1, p + REACH, at, pot[p, at])

    def finish(p, total, grad):
        return psi[p] * (total + co[C_T] * grad)

    spectra(span // 2, lambda t: None, begin, finish, ty_ref, tz, ccy_ref, cc_ref, (send_ref, keep_ref),
            lap, part, stack, freq)


def pack_kernel(n_space, terms, share_ref, *refs):
    count = sum(terms)
    outs, cells = refs[count:-1], refs[-1]
    piece, size = outs[0].shape[0], outs[0].shape[1]
    width = refs[0].shape[2]
    half = width // 2
    slab = lax.axis_index("space")
    chunks = [refs[sum(terms[:c]):sum(terms[:c + 1])] for c in range(len(terms))]
    total = 2 * sum(chunk[0].shape[0] for chunk in chunks)
    if total < size or piece * n_space > 3 * half:
        cells[...] = jnp.zeros_like(cells)
    low = lax.broadcasted_iota(jnp.int32, (half, LANES), 1) < LANES // 2
    x = 0
    for chunk in chunks:
        for i in range(chunk[0].shape[0]):
            for j in range(2):
                cells[pl.ds(x + j, width, stride=size), :] = sum(ref[i, j] for ref in chunk[1:]) + chunk[0][i, j]
            tail = sum(ref[i, 2] for ref in chunk[1:]) + chunk[0][i, 2]
            a, b = tail[:half], tail[half:]
            cells[pl.ds(width * size + x, half, stride=size), :] = jnp.where(low, a, pltpu.roll(b, LANES // 2, 1))
            cells[pl.ds(width * size + x + 1, half, stride=size), :] = jnp.where(low, pltpu.roll(a, LANES // 2, 1), b)
            x += 2
    for k in range(n_space):
        dest = lax.rem(slab + k, n_space)
        for r in range(piece):
            where = pl.multiple_of((dest * piece + r) * size, 8)
            outs[k][r] = cells[pl.ds(where, size), :]


def x_kernel(n_space, batches, share_ref, *refs):
    ins = refs[:batches * n_space]
    ah_ref, al_ref, bh_ref, bl_ref, mul_ref = refs[batches * n_space:batches * n_space + 5]
    outs = refs[batches * n_space + 5:-2]
    cells, back = refs[-2:]
    slab = lax.axis_index("space")
    rows, size_out = outs[0].shape[0], outs[0].shape[1]
    parts = len(outs) // n_space
    total = sum(ins[i * n_space].shape[1] for i in range(batches))
    for k in range(n_space):
        at = lax.rem(slab - k + n_space, n_space) * total
        for i in range(batches):
            ref = ins[i * n_space + k]
            size = ref.shape[1]
            for r in range(rows):
                cells[pl.ds(pl.multiple_of(at, 8), size), r * LANES:(r + 1) * LANES] = ref[r]
            at = at + size
    spec = mm3(ah_ref[...], al_ref[...], cells[...]) * mul_ref[...]
    back[...] = mm3(bh_ref[...], bl_ref[...], spec)
    for k in range(n_space):
        for h in range(parts):
            at = pl.multiple_of((lax.rem(slab + k, n_space) * parts + h) * size_out, 8)
            for r in range(rows):
                outs[h * n_space + k][r] = back[pl.ds(at, size_out), r * LANES:(r + 1) * LANES]


def y_kernel(n_space, width, share_ref, *refs):
    ins = refs[:n_space]
    wh_ref, wl_ref = refs[n_space:n_space + 2]
    outs = refs[n_space + 2:-4]
    cells, rows_ref, prod, mixed = refs[-4:]
    piece, count_x = ins[0].shape[0], ins[0].shape[1]
    n_band = len(outs)
    half = width // 2
    per_tile = LANES // width
    tiles = outs[0].shape[0] // width
    me, slab = lax.axis_index("band"), lax.axis_index("space")
    for k in range(n_space):
        src = lax.rem(slab - k + n_space, n_space)
        for r in range(piece):
            where = pl.multiple_of((src * piece + r) * count_x, 8)
            cells[pl.ds(where, count_x), :] = ins[k][r]
    for i in range(per_tile):
        for t in range(tiles):
            x = t * per_tile + i
            at = (i * tiles + t) * width
            if x >= count_x:
                rows_ref[pl.ds(at, width), :] = jnp.zeros((width, 2 * LANES), F32)
                continue
            tail = cells[pl.ds(width * count_x + x, half, stride=count_x), :]
            rows_ref[pl.ds(at, width), :LANES] = cells[pl.ds(x, width, stride=count_x), :]
            rows_ref[pl.ds(at, half), LANES:] = tail
            rows_ref[pl.ds(at + half, half), LANES:] = pltpu.roll(tail, LANES // 2, 1)
    prod[...] = mm3_right(rows_ref[...], wh_ref[...], wl_ref[...])
    size = tiles * width
    lane = lax.broadcasted_iota(jnp.int32, (size, LANES), 1)
    for b in range(n_band):
        tile, spot = divmod(b, per_tile)
        acc = jnp.zeros((size, LANES), F32)
        for i in range(per_tile):
            part = prod[pl.ds(i * size, size), tile * LANES:(tile + 1) * LANES]
            shift = (i - spot) * width % LANES
            if shift:
                part = pltpu.roll(part, shift, 1)
            acc = jnp.where((lane >= i * width) & (lane < (i + 1) * width), part, acc)
        mixed[b ^ me] = acc
    for p in range(n_band):
        outs[p][...] = mixed[p]


def z_kernel(n_band, share_ref, *refs):
    th_ref, tl_ref, out_ref, stack = refs[-4:]
    ins = refs[:-4]
    parts = len(ins) // n_band
    count_x, width = out_ref.shape[0], out_ref.shape[1]
    size = count_x // parts
    per_tile = LANES // width
    tiles = ins[0].shape[0] // width
    for h in range(parts):
        for p in range(n_band):
            block = lax.axis_index("band") ^ p
            for t in range(tiles):
                stack[h * tiles + t, block] = ins[h * n_band + p][t * width:(t + 1) * width]
    for h in range(parts):
        for t in range(tiles):
            cells = stack[h * tiles + t].reshape(n_band * width, LANES)
            plane = mm3_right(cells.T, th_ref[...], tl_ref[...])
            for i in range(per_tile):
                x = t * per_tile + i
                if x < size:
                    out_ref[h * size + x] = plane[i * width:(i + 1) * width]


def shape_of(*dims, dtype=F32):
    return jax.ShapeDtypeStruct(dims, dtype)


def shift_perm(count, k):
    return [(i, (i + k) % count) for i in range(count)]


def coefficients(shift, occupation, total_orbitals):
    delta = 5.5
    theta = shift + delta
    ratio = theta / delta
    w0 = 1.0 / ratio
    w1 = 1.0 / (2.0 * ratio - w0)
    w2 = 1.0 / (2.0 * ratio - w1)
    b1 = 2.0 * w1 / delta
    b2 = 2.0 * w2 / delta
    weight = occupation * (4.0 / total_orbitals)
    centre = -0.5 * 3.0 * COEFFS[0]
    co = [jnp.zeros_like(shift)] * 16
    co[C_SRC] = -1.0 / theta
    co[C_A] = w1 * w0 + b1 * theta - b1 * (shift + centre)
    co[C_B] = b1
    co[C_S] = 0.5 * b1 / DENOM
    co[C_D0] = weight * (1.0 - w2 * w0)
    co[C_G] = weight * (1.0 + w2 * w1 + w2 / w1 - b2 * (shift + centre))
    co[C_P] = weight * b2
    co[C_T] = weight * 0.5 * b2 / DENOM
    return jnp.stack(co)


def chunk_sizes(groups):
    first = -(-groups // 2)
    return [first, groups - first]


def ceil8(count):
    return -(-count // 8) * 8


def program_on_device(orbitals, occupations, shifts, perturbations, local_potential):
    count_x, n = orbitals.shape[1], orbitals.shape[2]
    n_band, n_space = lax.axis_size("band"), lax.axis_size("space")
    bits = n_band.bit_length() - 1
    assert orbitals.shape[0] == 1 and perturbations.shape[0] == 1 and n_band == 1 << bits
    assert 2 * (n - LANES) == LANES and count_x % 8 == 0 and count_x >= 5 * REACH
    band, slab = lax.axis_index("band"), lax.axis_index("space")
    orders = block_orders(n_band)
    share = jnp.asarray(orders)
    orb, pert, pot = orbitals[0], perturbations[0], local_potential
    width = n // n_band
    half = width // 2
    per_plane = n + n // 2
    wide = 2 * LANES
    smem = pl.BlockSpec(memory_space=pltpu.SMEM)
    vmem = pl.BlockSpec(memory_space=pltpu.VMEM)
    anywhere = pl.BlockSpec(memory_space=pl.ANY)
    dma = pltpu.SemaphoreType.DMA
    co = coefficients(shifts[0], occupations[0], n_band * orbitals.shape[0])

    base = cas_np(range(n), range(n), n)
    base_h, base_l = split_np(base)
    ring = circulant_np(n)
    ring_y = np.concatenate([ring, ring], axis=1)
    ty = np.concatenate([base_h, base_h, base_l], axis=1)
    whole = REACH * per_plane
    low, high = pl.pallas_call(
        edges_kernel,
        out_shape=[shape_of(whole + whole // 2, LANES)] * 2,
        in_specs=[smem, anywhere, anywhere],
        out_specs=[vmem] * 2,
        scratch_shapes=[
            pltpu.VMEM((2, REACH, n, n), BF16), pltpu.VMEM((2, REACH, n, n), F32),
            pltpu.VMEM((whole, LANES), F32), dma((2, 2)),
        ],
        name="edges", compiler_params=pltpu.CompilerParams(vmem_limit_bytes=12 * MIB),
    )(share, orb, pert)
    cores = [(b, b ^ 1) for b in range(n_band)]
    halos = []
    for cells, k in ((high, 1), (low, n_space - 1)):
        mine = lax.ppermute(cells, "space", shift_perm(n_space, k))
        other = lax.ppermute(mine[whole:], "band", cores)
        halos.append((mine, other))

    tables = (jnp.asarray(ring), jnp.asarray(ring_y), jnp.asarray(ty), jnp.asarray(base.reshape(n_band, width, n)))
    table_specs = [vmem] * 4

    def halves(pairs):
        return [shape_of(pairs, 3, n // 2, LANES)] * 2

    def stages():
        return [
            pltpu.VMEM((n, 3 * wide), BF16), pltpu.VMEM((UNROLL, 2 * n, n), BF16), pltpu.VMEM((UNROLL, n, n), F32),
            pltpu.VMEM((UNROLL, 3 * n, n), BF16), pltpu.VMEM((UNROLL, n, 3 * wide), BF16),
        ]

    chunks = chunk_sizes(count_x // REACH - 4)
    size_a = chunks[0] * REACH
    d1, *sent_a = pl.pallas_call(
        lambda *refs: first_kernel(n_band, *refs),
        out_shape=[shape_of(count_x, n, n)] + halves(size_a // 2),
        in_specs=[smem, smem] + [anywhere] * 3 + table_specs,
        out_specs=[anywhere, vmem, vmem],
        scratch_shapes=[
            pltpu.VMEM((count_x, n, n), BF16), pltpu.VMEM((count_x, n, n), F32),
            pltpu.VMEM((count_x, n, n), F32), pltpu.VMEM((count_x, n, n), F32), *stages(),
            dma((3, count_x // REACH)), dma((count_x // REACH,)),
        ],
        name="first_a", compiler_params=pltpu.CompilerParams(vmem_limit_bytes=52 * MIB),
    )(share, co, orb, pert, pot, *tables)

    def inner(start, count):
        return pl.pallas_call(
            lambda *refs: inner_kernel(n_band, start, *refs),
            out_shape=halves(count // 2),
            in_specs=[smem, smem] + [anywhere] * 4 + table_specs,
            out_specs=[vmem, vmem],
            scratch_shapes=[
                pltpu.VMEM((count, n, n), BF16), pltpu.VMEM((count, n, n), F32), pltpu.VMEM((count, n, n), F32),
                pltpu.VMEM((count + 2 * REACH, n, n), F32), *stages(), dma((4, count // 2)), dma((1,)),
            ],
            compiler_params=pltpu.CompilerParams(vmem_limit_bytes=28 * MIB),
        )(share, co, orb, pert, pot, d1, *tables)

    span = 3 * REACH

    def outer(side, halo):
        return pl.pallas_call(
            lambda *refs: boundary_kernel(n_band, side, *refs),
            out_shape=halves(span // 2),
            in_specs=[smem, smem] + [anywhere] * 4 + [vmem] * 2 + table_specs,
            out_specs=[vmem, vmem],
            scratch_shapes=[
                pltpu.VMEM((span, n, n), BF16), pltpu.VMEM((span, n, n), F32), pltpu.VMEM((span, n, n), F32),
                pltpu.VMEM((span, n, n), F32), pltpu.VMEM((span, n, n), F32), pltpu.VMEM((5 * REACH, n, n), F32),
                pltpu.VMEM((whole, LANES), F32), *stages(), dma((4,)),
            ],
            compiler_params=pltpu.CompilerParams(vmem_limit_bytes=28 * MIB),
        )(share, co, orb, pert, pot, d1, *halo, *tables)

    def halving(send, keep):
        for stage in range(bits):
            perm = [(b, partner(b, stage, bits)) for b in range(n_band)]
            got = lax.ppermute(send, "band", perm)
            if stage < bits - 1:
                cut = keep.shape[2] // 2
                send, keep = keep[:, :, :cut] + got[:, :, :cut], keep[:, :, cut:] + got[:, :, cut:]
        return [keep, got]

    def direct(send, keep):
        perm = [(b, partner(b, 0, bits)) for b in range(n_band)]
        got = lax.ppermute(send, "band", perm)
        blocks = []
        for m in range(n_band // 2):
            rows = slice(m * width, (m + 1) * width)
            block = keep[:, :, rows] + got[:, :, rows]
            if m < n_band // 2 - 1:
                perm = [(b, int(orders[b, n_band // 2 + m])) for b in range(n_band)]
                block = lax.ppermute(block, "band", perm)
            blocks.append(block)
        return blocks

    piece = -(-3 * half // n_space)

    def to_columns(chunks):
        size = ceil8(2 * sum(chunk[0].shape[0] for chunk in chunks))
        blocks = pl.pallas_call(
            lambda *refs: pack_kernel(n_space, [len(chunk) for chunk in chunks], *refs),
            out_shape=[shape_of(piece, size, LANES)] * n_space,
            in_specs=[smem] + [vmem] * sum(len(chunk) for chunk in chunks),
            out_specs=[vmem] * n_space,
            scratch_shapes=[pltpu.VMEM((piece * n_space * size, LANES), F32)],
            compiler_params=pltpu.CompilerParams(vmem_limit_bytes=12 * MIB),
        )(share, *(ref for chunk in chunks for ref in chunk))
        return [lax.ppermute(blocks[k], "space", shift_perm(n_space, k)) if k else blocks[0] for k in range(n_space)]

    inside = np.arange(2 * REACH, count_x - 2 * REACH)
    planes = {
        "a": inside[:size_a],
        "b": inside[size_a:],
        "p": np.arange(-REACH, 2 * REACH),
        "q": np.arange(count_x - 2 * REACH, count_x + REACH),
    }
    sums = [
        direct(*sent_a),
        direct(*inner(2 * REACH + size_a, chunks[1] * REACH)),
        halving(*outer(0, halos[0])),
        halving(*outer(1, halos[1])),
    ]
    batches = (("a", "b"), ("p", "q"))
    at = dict(zip(planes, sums))
    received = [to_columns([at[name] for name in names]) for names in batches]

    a_parts = []
    for s in range(n_space):
        for names in batches:
            at = np.concatenate([planes[name] for name in names])
            block = base[:, (s * count_x + at) % n]
            a_parts.append(np.pad(block, ((0, 0), (0, ceil8(len(at)) - len(at)))))
    a_h, a_l = split_np(np.concatenate(a_parts, axis=1))

    def folded(values):
        return jnp.minimum(values, n - values).astype(F32)

    row = slab * piece + jnp.arange(piece, dtype=jnp.int32)[:, None]
    lane = jnp.arange(LANES, dtype=jnp.int32)[None, :]
    is_tail = row >= width
    ky = jnp.where(is_tail, LANES + lane % (LANES // 2), lane)
    kz_in = jnp.where(is_tail, row - width + jnp.where(lane < LANES // 2, 0, half), row)
    kz = jnp.clip(band * width + kz_in, 0, n)
    squares = (folded(ky) ** 2 + folded(kz) ** 2).reshape(1, piece * LANES)
    kx = folded(jnp.arange(n, dtype=jnp.int32))
    multiplier = (256.0 / float(n) ** 3) / jnp.sqrt(squares + (kx ** 2)[:, None] + 1.0)

    n_parts = 1
    part_x = count_x // n_parts
    base_h, base_l = jnp.asarray(base_h), jnp.asarray(base_l)
    backs = pl.pallas_call(
        lambda *refs: x_kernel(n_space, len(received), *refs),
        out_shape=[shape_of(piece, part_x, LANES)] * (n_space * n_parts),
        in_specs=[smem] + [vmem] * (len(received) * n_space + 5),
        out_specs=[vmem] * (n_space * n_parts),
        scratch_shapes=[
            pltpu.VMEM((a_h.shape[1], piece * LANES), F32), pltpu.VMEM((n, piece * LANES), F32),
        ],
        name="along_x", compiler_params=pltpu.CompilerParams(vmem_limit_bytes=20 * MIB),
    )(share, *(ref for blocks in received for ref in blocks), jnp.asarray(a_h), jnp.asarray(a_l), base_h, base_l, multiplier)
    per_tile = LANES // width
    tiles = -(-part_x // per_tile)
    y_tiles = -(-n_band // per_tile)
    w_table = np.zeros((wide, y_tiles * LANES), np.float32)
    for b in range(n_band):
        t, spot = divmod(b, per_tile)
        w_table[:n, t * LANES + spot * width:t * LANES + (spot + 1) * width] = base[:, b * width:(b + 1) * width]
    w_h, w_l = split_np(w_table)
    rows_y = per_tile * tiles * width
    pieces = []
    for h in range(n_parts):
        blocks = backs[h * n_space:(h + 1) * n_space]
        slabs = [lax.ppermute(blocks[k], "space", shift_perm(n_space, k)) if k else blocks[0] for k in range(n_space)]
        by_rows = pl.pallas_call(
            lambda *refs: y_kernel(n_space, width, *refs),
            out_shape=[shape_of(tiles * width, LANES)] * n_band,
            in_specs=[smem] + [vmem] * (n_space + 2),
            out_specs=[vmem] * n_band,
            scratch_shapes=[
                pltpu.VMEM((piece * n_space * part_x, LANES), F32),
                pltpu.VMEM((rows_y, wide), F32),
                pltpu.VMEM((rows_y, y_tiles * LANES), F32),
                pltpu.VMEM((n_band, tiles * width, LANES), F32),
            ],
            compiler_params=pltpu.CompilerParams(vmem_limit_bytes=24 * MIB),
        )(share, *slabs, jnp.asarray(w_h), jnp.asarray(w_l))
        pieces += [
            lax.ppermute(by_rows[p], "band", [(b, b ^ p) for b in range(n_band)])
            if p else by_rows[0]
            for p in range(n_band)
        ]

    out = pl.pallas_call(
        lambda *refs: z_kernel(n_band, *refs),
        out_shape=shape_of(count_x, width, n),
        in_specs=[smem] + [vmem] * (n_parts * n_band + 2),
        out_specs=vmem,
        scratch_shapes=[pltpu.VMEM((n_parts * tiles, n_band, width, LANES), F32)],
        name="along_z", compiler_params=pltpu.CompilerParams(vmem_limit_bytes=16 * MIB),
    )(share, *pieces, base_h, base_l)
    return out[None]


def solution(mesh):
    in_specs = (
        P("band", "space", None, None),
        P("band"),
        P("band"),
        P(None, "space", None, None),
        P("space", None, None),
    )
    out_specs = P(None, "space", "band", None)
    return jax.shard_map(program_on_device, mesh=mesh, in_specs=in_specs, out_specs=out_specs, check_vma=False)
```

profile of v0, /device:TPU:0, one launch (start us, length us, event | category | flops | bytes accessed | tf_op | source)
XLA Modules:
  0.0 195.2 jit_solution(14544888614747448142)
XLA Ops:
  0.0 3.7 %copy-done = f32[1,48,192,192]{3,2,1,0:T(8,128)S(1)} copy-done((f32[1,48,192,192]{3,2,1,0:T(8,128)S(1)}, f32[1,48,192,192]{3,2,1,0:T(8,128)}, u32[]{:S(2)}) %copy-start) | copy-done | bytes 7077912
  6.7 2.6 %edges.1 = (f32[1728,128]{1,0:T(8,128)}, f32[1728,128]{1,0:T(8,128)}) custom-call(s32[8,8]{1,0:T(8,128)S(1)} %copy-done.14, bf16[48,192,192]{2,1,0:T(8,128)(2,1)S(1)} %bitcast.28, f32[48,192,192]{2,1,0:T(8,128)S(1)} %bitcast.21), custom_call_target="tpu_custom_call" | custom-call | tf_op jit(solution)/shard_map/edges/pallas_call | solution.py:542
  9.3 3.1 %collective-permute-start.11 = (f32[1728,128]{1,0:T(8,128)}, f32[1728,128]{1,0:T(8,128)}, u32[]{:S(2)}, u32[]{:S(2)}) collective-permute-start(f32[1728,128]{1,0:T(8,128)} %get-tuple-element.45), channel_id=1, source_target_pairs={{0,1},{1,2},{2,3},{3,0},{4,5},{5,6},{6,7},{7,4},{8,9},{9,10},{10,1... | collective-permute-start | bytes 2654216 | tf_op jit(solution)/shard_map/ppermute | solution.py:556
  16.2 22.1 %first_a.1 = (f32[48,192,192]{2,1,0:T(8,128)}, f32[8,3,96,128]{3,2,1,0:T(8,128)}, f32[8,3,96,128]{3,2,1,0:T(8,128)}) custom-call(s32[8,8]{1,0:T(8,128)S(1)} %copy-done.15, f32[16]{0:T(128)S(1)} %stack.35.refs_1_, bf16[48,192,192]{2,1,0:T(8,128)(2,1)} %bitcast.27, f32[48,192,192]{2,1,0:T(8,128)} %bitcast.20, f32[48,192,192]{2,1,0:T(8,128)} %refs_4_.7, ...), custom_call_target="tpu_custom_call" | custom-call | tf_op jit(solution)/shard_map/first_a/pallas_call | solution.py:574
  38.4 3.7 %copy-done.2 = f32[48,192,192]{2,1,0:T(8,128)S(1)} copy-done((f32[48,192,192]{2,1,0:T(8,128)S(1)}, f32[48,192,192]{2,1,0:T(8,128)}, u32[]{:S(2)}) %copy-start.2) | copy-done | bytes 7077912
  44.4 14.3 %shard_map.154 = (f32[8,3,96,128]{3,2,1,0:T(8,128)}, f32[8,3,96,128]{3,2,1,0:T(8,128)S(1)}) custom-call(s32[8,8]{1,0:T(8,128)S(1)} %copy-done.15, f32[16]{0:T(128)S(1)} %stack.35.refs_1_, bf16[48,192,192]{2,1,0:T(8,128)(2,1)S(1)} %bitcast.29, f32[48,192,192]{2,1,0:T(8,128)S(1)} %bitcast.24, f32[48,192,192]{2,1,0:T(8,128)S(1)} %copy-done.2, ...), custom_call_target="tpu_custom_call" | custom-call | tf_op jit(solution)/shard_map/pallas_call | solution.py:588
  62.5 10.7 %shard_map.156 = (f32[6,3,96,128]{3,2,1,0:T(8,128)}, f32[6,3,96,128]{3,2,1,0:T(8,128)S(1)}) custom-call(s32[8,8]{1,0:T(8,128)S(1)} %copy-done.15, f32[16]{0:T(128)S(1)} %stack.35.refs_1_, bf16[48,192,192]{2,1,0:T(8,128)(2,1)S(1)} %bitcast.30, f32[48,192,192]{2,1,0:T(8,128)S(1)} %bitcast.25, f32[48,192,192]{2,1,0:T(8,128)} %refs_4_.7, ...), custom_call_target="tpu_custom_call" | custom-call | tf_op jit(solution)/shard_map/pallas_call | solution.py:603
  74.5 3.7 %copy-done.1 = f32[1,48,192,192]{3,2,1,0:T(8,128)S(1)} copy-done((f32[1,48,192,192]{3,2,1,0:T(8,128)S(1)}, f32[1,48,192,192]{3,2,1,0:T(8,128)}, u32[]{:S(2)}) %copy-start.1) | copy-done | bytes 7077912
  80.5 10.1 %shard_map.157 = (f32[6,3,96,128]{3,2,1,0:T(8,128)S(1)}, f32[6,3,96,128]{3,2,1,0:T(8,128)S(1)}) custom-call(s32[8,8]{1,0:T(8,128)S(1)} %copy-done.15, f32[16]{0:T(128)S(1)} %stack.35.refs_1_, bf16[48,192,192]{2,1,0:T(8,128)(2,1)S(1)} %bitcast.31, f32[48,192,192]{2,1,0:T(8,128)S(1)} %bitcast.26, f32[48,192,192]{2,1,0:T(8,128)} %refs_4_.7, ...), custom_call_target="tpu_custom_call" | custom-call | tf_op jit(solution)/shard_map/pallas_call | solution.py:603
  92.5 2.7 %collective-permute-start.1 = (f32[8,3,24,128]{3,2,1,0:T(8,128)S(1)}, f32[8,3,24,128]{3,2,1,0:T(8,128)S(1)}, u32[]{:S(2)}, u32[]{:S(2)}) collective-permute-start(f32[8,3,24,128]{3,2,1,0:T(8,128)S(1)} %get-tuple-element.74), channel_id=1, source_target_pairs={{0,24},{4,28},{8,16},{12,20},{16,8},{20,12},{24,0},{28,4},{1,25},{... | collective-permute-start | bytes 884744 | tf_op jit(solution)/shard_map/ppermute | solution.py:634
  97.5 2.7 %collective-permute-start.5 = (f32[8,3,24,128]{3,2,1,0:T(8,128)S(1)}, f32[8,3,24,128]{3,2,1,0:T(8,128)S(1)}, u32[]{:S(2)}, u32[]{:S(2)}) collective-permute-start(f32[8,3,24,128]{3,2,1,0:T(8,128)S(1)} %get-tuple-element.70), channel_id=1, source_target_pairs={{0,24},{4,28},{8,16},{12,20},{16,8},{20,12},{24,0},{28,4},{1,25},{... | collective-permute-start | bytes 884744 | tf_op jit(solution)/shard_map/ppermute | solution.py:634
  100.4 3.0 %collective-permute-done.1.refs_1_ = f32[8,3,24,128]{3,2,1,0:T(8,128)S(1)} collective-permute-done((f32[8,3,24,128]{3,2,1,0:T(8,128)S(1)}, f32[8,3,24,128]{3,2,1,0:T(8,128)S(1)}, u32[]{:S(2)}, u32[]{:S(2)}) %collective-permute-start.1) | collective-permute-done | bytes 294944 | tf_op jit(solution)/shard_map/ppermute | solution.py:634
  105.1 4.9 %collective-permute-done.2.refs_2_ = f32[8,3,24,128]{3,2,1,0:T(8,128)S(1)} collective-permute-done((f32[8,3,24,128]{3,2,1,0:T(8,128)S(1)}, f32[8,3,24,128]{3,2,1,0:T(8,128)S(1)}, u32[]{:S(2)}, u32[]{:S(2)}) %collective-permute-start.2) | collective-permute-done | bytes 294944 | tf_op jit(solution)/shard_map/ppermute | solution.py:634
  112.5 3.6 %collective-permute-done.5.refs_5_ = f32[8,3,24,128]{3,2,1,0:T(8,128)S(1)} collective-permute-done((f32[8,3,24,128]{3,2,1,0:T(8,128)S(1)}, f32[8,3,24,128]{3,2,1,0:T(8,128)S(1)}, u32[]{:S(2)}, u32[]{:S(2)}) %collective-permute-start.5) | collective-permute-done | bytes 294944 | tf_op jit(solution)/shard_map/ppermute | solution.py:634
  116.1 5.9 %collective-permute-done.6.refs_6_ = f32[8,3,24,128]{3,2,1,0:T(8,128)S(1)} collective-permute-done((f32[8,3,24,128]{3,2,1,0:T(8,128)S(1)}, f32[8,3,24,128]{3,2,1,0:T(8,128)S(1)}, u32[]{:S(2)}, u32[]{:S(2)}) %collective-permute-start.6) | collective-permute-done | bytes 294944 | tf_op jit(solution)/shard_map/ppermute | solution.py:634
  123.3 3.4 %collective-permute-done.14 = f32[6,3,48,128]{3,2,1,0:T(8,128)S(1)} collective-permute-done((f32[6,3,48,128]{3,2,1,0:T(8,128)S(1)}, f32[6,3,48,128]{3,2,1,0:T(8,128)S(1)}, u32[]{:S(2)}, u32[]{:S(2)}) %collective-permute-start.14) | collective-permute-done | bytes 442400 | tf_op jit(solution)/shard_map/ppermute | solution.py:619
  127.1 6.5 %collective-permute-done.19 = f32[6,3,48,128]{3,2,1,0:T(8,128)S(1)} collective-permute-done((f32[6,3,48,128]{3,2,1,0:T(8,128)S(1)}, f32[6,3,48,128]{3,2,1,0:T(8,128)S(1)}, u32[]{:S(2)}, u32[]{:S(2)}) %collective-permute-start.19) | collective-permute-done | bytes 442400 | tf_op jit(solution)/shard_map/ppermute | solution.py:619
  136.0 3.8 %collective-permute-done.20.refs_4_ = f32[6,3,24,128]{3,2,1,0:T(8,128)S(1)} collective-permute-done((f32[6,3,24,128]{3,2,1,0:T(8,128)S(1)}, f32[6,3,24,128]{3,2,1,0:T(8,128)S(1)}, u32[]{:S(2)}, u32[]{:S(2)}) %collective-permute-start.20) | collective-permute-done | bytes 221216 | tf_op jit(solution)/shard_map/ppermute | solution.py:619
  144.6 3.2 %collective-permute-done.21.refs_6_ = f32[9,24,128]{2,1,0:T(8,128)S(1)} collective-permute-done((f32[9,24,128]{2,1,0:T(8,128)S(1)}, f32[9,24,128]{2,1,0:T(8,128)S(1)}, u32[]{:S(2)}, u32[]{:S(2)}) %collective-permute-start.21) | collective-permute-done | bytes 110624 | tf_op jit(solution)/shard_map/ppermute | solution.py:650
  147.9 5.4 %collective-permute-done.22.refs_7_ = f32[9,24,128]{2,1,0:T(8,128)S(1)} collective-permute-done((f32[9,24,128]{2,1,0:T(8,128)S(1)}, f32[9,24,128]{2,1,0:T(8,128)S(1)}, u32[]{:S(2)}, u32[]{:S(2)}) %collective-permute-start.22) | collective-permute-done | bytes 110624 | tf_op jit(solution)/shard_map/ppermute | solution.py:650
  155.4 2.9 %collective-permute-start.24 = (f32[9,48,128]{2,1,0:T(8,128)S(1)}, f32[9,48,128]{2,1,0:T(8,128)S(1)}, u32[]{:S(2)}, u32[]{:S(2)}) collective-permute-start(f32[9,48,128]{2,1,0:T(8,128)S(1)} %get-tuple-element.56), channel_id=1, source_target_pairs={{0,1},{1,2},{2,3},{3,0},{4,5},{5,6},{6,7},{7,4},{8,9},{9,10},{10,1... | collective-permute-start | bytes 663560 | tf_op jit(solution)/shard_map/ppermute | solution.py:715
  160.9 5.9 %collective-permute-done.24.refs_2_ = f32[9,48,128]{2,1,0:T(8,128)S(1)} collective-permute-done((f32[9,48,128]{2,1,0:T(8,128)S(1)}, f32[9,48,128]{2,1,0:T(8,128)S(1)}, u32[]{:S(2)}, u32[]{:S(2)}) %collective-permute-start.24) | collective-permute-done | bytes 221216 | tf_op jit(solution)/shard_map/ppermute | solution.py:715
  166.7 8.8 %collective-permute-done.25.refs_3_ = f32[9,48,128]{2,1,0:T(8,128)S(1)} collective-permute-done((f32[9,48,128]{2,1,0:T(8,128)S(1)}, f32[9,48,128]{2,1,0:T(8,128)S(1)}, u32[]{:S(2)}, u32[]{:S(2)}) %collective-permute-start.25) | collective-permute-done | bytes 221216 | tf_op jit(solution)/shard_map/ppermute | solution.py:715
  186.0 6.7 %collective-permute-done.31.refs_6_ = f32[240,128]{1,0:T(8,128)S(1)} collective-permute-done((f32[240,128]{1,0:T(8,128)S(1)}, f32[240,128]{1,0:T(8,128)S(1)}, u32[]{:S(2)}, u32[]{:S(2)}) %collective-permute-start.31) | collective-permute-done | bytes 122912 | tf_op jit(solution)/shard_map/ppermute | solution.py:730
  (123 shorter events, 50.1 us)
Async XLA Ops:
  9.3 50.0 %collective-permute-start.11 = (f32[1728,128]{1,0:T(8,128)}, f32[1728,128]{1,0:T(8,128)}, u32[]{:S(2)}, u32[]{:S(2)}) collective-permute-start(f32[1728,128]{1,0:T(8,128)} %get-tuple-element.45), channel_id=1, source_target_pairs={{0,1},{1,2},{2,3},{3,0},{4,5},{5,6},{6,7},{7,4},{8,9},{9,10},{10,1... | collective-permute-start | bytes 2654216 | tf_op jit(solution)/shard_map/ppermute | solution.py:556
  12.4 48.2 %collective-permute-start.16 = (f32[1728,128]{1,0:T(8,128)}, f32[1728,128]{1,0:T(8,128)}, u32[]{:S(2)}, u32[]{:S(2)}) collective-permute-start(f32[1728,128]{1,0:T(8,128)} %get-tuple-element.48), channel_id=1, source_target_pairs={{0,3},{1,0},{2,1},{3,2},{4,7},{5,4},{6,5},{7,6},{8,11},{9,8},{10,9... | collective-permute-start | bytes 2654216 | tf_op jit(solution)/shard_map/ppermute | solution.py:556
  38.3 52.7 %collective-permute-start = (f32[8,3,96,128]{3,2,1,0:T(8,128)}, f32[8,3,96,128]{3,2,1,0:T(8,128)}, u32[]{:S(2)}, u32[]{:S(2)}) collective-permute-start(f32[8,3,96,128]{3,2,1,0:T(8,128)} %get-tuple-element.37), channel_id=1, source_target_pairs={{0,4},{4,0},{8,12},{12,8},{16,20},{20,16},{24,28},{28,24},{1,5},{5... | collective-permute-start | bytes 3538952 | tf_op jit(solution)/shard_map/ppermute | solution.py:627
  58.8 37.0 %collective-permute-start.4 = (f32[8,3,96,128]{3,2,1,0:T(8,128)}, f32[8,3,96,128]{3,2,1,0:T(8,128)}, u32[]{:S(2)}, u32[]{:S(2)}) collective-permute-start(f32[8,3,96,128]{3,2,1,0:T(8,128)} %get-tuple-element.40), channel_id=1, source_target_pairs={{0,4},{4,0},{8,12},{12,8},{16,20},{20,16},{24,28},{28,24},{1,5},{5... | collective-permute-start | bytes 3538952 | tf_op jit(solution)/shard_map/ppermute | solution.py:627
  62.3 12.2 %collective-permute-start.17 = (f32[576,128]{1,0:T(8,128)}, f32[576,128]{1,0:T(8,128)S(1)}, u32[]{:S(2)}, u32[]{:S(2)}) collective-permute-start(f32[576,128]{1,0:T(8,128)} %slice.151), channel_id=1, source_target_pairs={{0,4},{4,0},{8,12},{12,8},{16,20},{20,16},{24,28},{28,24},{1,5},{5... | collective-permute-start | bytes 884744 | tf_op jit(solution)/shard_map/ppermute | solution.py:557
  74.2 23.3 %collective-permute-start.13 = (f32[6,3,96,128]{3,2,1,0:T(8,128)}, f32[6,3,96,128]{3,2,1,0:T(8,128)S(1)}, u32[]{:S(2)}, u32[]{:S(2)}) collective-permute-start(f32[6,3,96,128]{3,2,1,0:T(8,128)} %get-tuple-element.47), channel_id=1, source_target_pairs={{0,4},{4,0},{8,12},{12,8},{16,20},{20,16},{24,28},{28,24},{1,5},{5... | collective-permute-start | bytes 2654216 | tf_op jit(solution)/shard_map/ppermute | solution.py:619
  90.7 19.6 %collective-permute-start.18 = (f32[6,3,96,128]{3,2,1,0:T(8,128)S(1)}, f32[6,3,96,128]{3,2,1,0:T(8,128)S(1)}, u32[]{:S(2)}, u32[]{:S(2)}) collective-permute-start(f32[6,3,96,128]{3,2,1,0:T(8,128)S(1)} %get-tuple-element.50), channel_id=1, source_target_pairs={{0,4},{4,0},{8,12},{12,8},{16,20},{20,16},{24,28},{28,24},{1,5},{5... | collective-permute-start | bytes 2654216 | tf_op jit(solution)/shard_map/ppermute | solution.py:619
  92.5 10.9 %collective-permute-start.1 = (f32[8,3,24,128]{3,2,1,0:T(8,128)S(1)}, f32[8,3,24,128]{3,2,1,0:T(8,128)S(1)}, u32[]{:S(2)}, u32[]{:S(2)}) collective-permute-start(f32[8,3,24,128]{3,2,1,0:T(8,128)S(1)} %get-tuple-element.74), channel_id=1, source_target_pairs={{0,24},{4,28},{8,16},{12,20},{16,8},{20,12},{24,0},{28,4},{1,25},{... | collective-permute-start | bytes 884744 | tf_op jit(solution)/shard_map/ppermute | solution.py:634
  95.2 14.7 %collective-permute-start.2 = (f32[8,3,24,128]{3,2,1,0:T(8,128)S(1)}, f32[8,3,24,128]{3,2,1,0:T(8,128)S(1)}, u32[]{:S(2)}, u32[]{:S(2)}) collective-permute-start(f32[8,3,24,128]{3,2,1,0:T(8,128)S(1)} %get-tuple-element.73), channel_id=1, source_target_pairs={{0,8},{4,20},{8,0},{12,28},{16,24},{20,4},{24,16},{28,12},{1,9},{5... | collective-permute-start | bytes 884744 | tf_op jit(solution)/shard_map/ppermute | solution.py:634
  95.7 16.4 %collective-permute-start.3 = (f32[8,3,24,128]{3,2,1,0:T(8,128)S(1)}, f32[8,3,24,128]{3,2,1,0:T(8,128)S(1)}, u32[]{:S(2)}, u32[]{:S(2)}) collective-permute-start(f32[8,3,24,128]{3,2,1,0:T(8,128)S(1)} %get-tuple-element.72), channel_id=1, source_target_pairs={{0,16},{4,12},{8,24},{12,4},{16,0},{20,28},{24,8},{28,20},{1,17},{... | collective-permute-start | bytes 884744 | tf_op jit(solution)/shard_map/ppermute | solution.py:634
  97.5 18.5 %collective-permute-start.5 = (f32[8,3,24,128]{3,2,1,0:T(8,128)S(1)}, f32[8,3,24,128]{3,2,1,0:T(8,128)S(1)}, u32[]{:S(2)}, u32[]{:S(2)}) collective-permute-start(f32[8,3,24,128]{3,2,1,0:T(8,128)S(1)} %get-tuple-element.70), channel_id=1, source_target_pairs={{0,24},{4,28},{8,16},{12,20},{16,8},{20,12},{24,0},{28,4},{1,25},{... | collective-permute-start | bytes 884744 | tf_op jit(solution)/shard_map/ppermute | solution.py:634
  103.4 18.5 %collective-permute-start.6 = (f32[8,3,24,128]{3,2,1,0:T(8,128)S(1)}, f32[8,3,24,128]{3,2,1,0:T(8,128)S(1)}, u32[]{:S(2)}, u32[]{:S(2)}) collective-permute-start(f32[8,3,24,128]{3,2,1,0:T(8,128)S(1)} %get-tuple-element.69), channel_id=1, source_target_pairs={{0,8},{4,20},{8,0},{12,28},{16,24},{20,4},{24,16},{28,12},{1,9},{5... | collective-permute-start | bytes 884744 | tf_op jit(solution)/shard_map/ppermute | solution.py:634
  109.9 12.0 %collective-permute-start.7 = (f32[8,3,24,128]{3,2,1,0:T(8,128)S(1)}, f32[8,3,24,128]{3,2,1,0:T(8,128)S(1)}, u32[]{:S(2)}, u32[]{:S(2)}) collective-permute-start(f32[8,3,24,128]{3,2,1,0:T(8,128)S(1)} %get-tuple-element.68), channel_id=1, source_target_pairs={{0,16},{4,12},{8,24},{12,4},{16,0},{20,28},{24,8},{28,20},{1,17},{... | collective-permute-start | bytes 884744 | tf_op jit(solution)/shard_map/ppermute | solution.py:634
  110.3 16.4 %collective-permute-start.14 = (f32[6,3,48,128]{3,2,1,0:T(8,128)S(1)}, f32[6,3,48,128]{3,2,1,0:T(8,128)S(1)}, u32[]{:S(2)}, u32[]{:S(2)}) collective-permute-start(f32[6,3,48,128]{3,2,1,0:T(8,128)S(1)} %get-tuple-element.78), channel_id=1, source_target_pairs={{0,8},{4,20},{8,0},{12,28},{16,24},{20,4},{24,16},{28,12},{1,9},{5... | collective-permute-start | bytes 1327112 | tf_op jit(solution)/shard_map/ppermute | solution.py:619
  112.1 21.6 %collective-permute-start.19 = (f32[6,3,48,128]{3,2,1,0:T(8,128)S(1)}, f32[6,3,48,128]{3,2,1,0:T(8,128)S(1)}, u32[]{:S(2)}, u32[]{:S(2)}) collective-permute-start(f32[6,3,48,128]{3,2,1,0:T(8,128)S(1)} %get-tuple-element.76), channel_id=1, source_target_pairs={{0,8},{4,20},{8,0},{12,28},{16,24},{20,4},{24,16},{28,12},{1,9},{5... | collective-permute-start | bytes 1327112 | tf_op jit(solution)/shard_map/ppermute | solution.py:619
  123.2 19.6 %collective-permute-start.8 = (f32[9,32,128]{2,1,0:T(8,128)S(1)}, f32[9,32,128]{2,1,0:T(8,128)S(1)}, u32[]{:S(2)}, u32[]{:S(2)}) collective-permute-start(f32[9,32,128]{2,1,0:T(8,128)S(1)} %get-tuple-element.42), channel_id=1, source_target_pairs={{0,1},{1,2},{2,3},{3,0},{4,5},{5,6},{6,7},{7,4},{8,9},{9,10},{10,1... | collective-permute-start | bytes 442376 | tf_op jit(solution)/shard_map/ppermute | solution.py:650
  133.9 10.7 %collective-permute-start.9 = (f32[9,32,128]{2,1,0:T(8,128)S(1)}, f32[9,32,128]{2,1,0:T(8,128)S(1)}, u32[]{:S(2)}, u32[]{:S(2)}) collective-permute-start(f32[9,32,128]{2,1,0:T(8,128)S(1)} %get-tuple-element.43), channel_id=1, source_target_pairs={{0,2},{1,3},{2,0},{3,1},{4,6},{5,7},{6,4},{7,5},{8,10},{9,11},{10,... | collective-permute-start | bytes 442376 | tf_op jit(solution)/shard_map/ppermute | solution.py:650
  140.6 12.7 %collective-permute-start.22 = (f32[9,24,128]{2,1,0:T(8,128)S(1)}, f32[9,24,128]{2,1,0:T(8,128)S(1)}, u32[]{:S(2)}, u32[]{:S(2)}) collective-permute-start(f32[9,24,128]{2,1,0:T(8,128)S(1)} %get-tuple-element.53), channel_id=1, source_target_pairs={{0,2},{1,3},{2,0},{3,1},{4,6},{5,7},{6,4},{7,5},{8,10},{9,11},{10,... | collective-permute-start | bytes 331784 | tf_op jit(solution)/shard_map/ppermute | solution.py:650
  142.8 10.4 %collective-permute-start.23 = (f32[9,24,128]{2,1,0:T(8,128)S(1)}, f32[9,24,128]{2,1,0:T(8,128)S(1)}, u32[]{:S(2)}, u32[]{:S(2)}) collective-permute-start(f32[9,24,128]{2,1,0:T(8,128)S(1)} %get-tuple-element.54), channel_id=1, source_target_pairs={{0,3},{1,0},{2,1},{3,2},{4,7},{5,4},{6,5},{7,6},{8,11},{9,8},{10,9... | collective-permute-start | bytes 331784 | tf_op jit(solution)/shard_map/ppermute | solution.py:650
  155.4 11.3 %collective-permute-start.24 = (f32[9,48,128]{2,1,0:T(8,128)S(1)}, f32[9,48,128]{2,1,0:T(8,128)S(1)}, u32[]{:S(2)}, u32[]{:S(2)}) collective-permute-start(f32[9,48,128]{2,1,0:T(8,128)S(1)} %get-tuple-element.56), channel_id=1, source_target_pairs={{0,1},{1,2},{2,3},{3,0},{4,5},{5,6},{6,7},{7,4},{8,9},{9,10},{10,1... | collective-permute-start | bytes 663560 | tf_op jit(solution)/shard_map/ppermute | solution.py:715
  158.3 17.2 %collective-permute-start.25 = (f32[9,48,128]{2,1,0:T(8,128)S(1)}, f32[9,48,128]{2,1,0:T(8,128)S(1)}, u32[]{:S(2)}, u32[]{:S(2)}) collective-permute-start(f32[9,48,128]{2,1,0:T(8,128)S(1)} %get-tuple-element.57), channel_id=1, source_target_pairs={{0,2},{1,3},{2,0},{3,1},{4,6},{5,7},{6,4},{7,5},{8,10},{9,11},{10,... | collective-permute-start | bytes 663560 | tf_op jit(solution)/shard_map/ppermute | solution.py:715
  160.9 14.7 %collective-permute-start.26 = (f32[9,48,128]{2,1,0:T(8,128)S(1)}, f32[9,48,128]{2,1,0:T(8,128)S(1)}, u32[]{:S(2)}, u32[]{:S(2)}) collective-permute-start(f32[9,48,128]{2,1,0:T(8,128)S(1)} %get-tuple-element.58), channel_id=1, source_target_pairs={{0,3},{1,0},{2,1},{3,2},{4,7},{5,4},{6,5},{7,6},{8,11},{9,8},{10,9... | collective-permute-start | bytes 663560 | tf_op jit(solution)/shard_map/ppermute | solution.py:715
  181.1 11.5 %collective-permute-start.31 = (f32[240,128]{1,0:T(8,128)S(1)}, f32[240,128]{1,0:T(8,128)S(1)}, u32[]{:S(2)}, u32[]{:S(2)}) collective-permute-start(f32[240,128]{1,0:T(8,128)S(1)} %get-tuple-element.64), channel_id=1, source_target_pairs={{0,20},{4,16},{8,28},{12,24},{16,4},{20,0},{24,12},{28,8},{1,21},{... | collective-permute-start | bytes 368648 | tf_op jit(solution)/shard_map/ppermute | solution.py:730
  181.5 11.2 %collective-permute-start.32 = (f32[240,128]{1,0:T(8,128)S(1)}, f32[240,128]{1,0:T(8,128)S(1)}, u32[]{:S(2)}, u32[]{:S(2)}) collective-permute-start(f32[240,128]{1,0:T(8,128)S(1)} %get-tuple-element.65), channel_id=1, source_target_pairs={{0,24},{4,28},{8,16},{12,20},{16,8},{20,12},{24,0},{28,4},{1,25},{... | collective-permute-start | bytes 368648 | tf_op jit(solution)/shard_map/ppermute | solution.py:730
  (36 other events, 374.6 us)
where the time goes:
time: 199 us; the launch traced here: 195 us
  Pallas kernels  68.9 us (35%)
  waiting for transfers between devices  61.8 us (31%)
  starting transfers between devices  36.4 us (18%)
  local copies, waits for them, and re-layouts  22.5 us (11%)
  other arithmetic  3.6 us (2%)
    pallas_call x1, Pallas kernels, program_on_device(): pl.pallas_call(lambda *refs: first_kernel(n_band, *refs), out_shape=[shap...  22.1 us
    pallas_call x2, Pallas kernels, outer(): pl.pallas_call(lambda *refs: boundary_kernel(n_band, side, *refs), out_sh...  20.9 us
    unnamed x52, local copies, waits for them, and re-layouts  19.8 us
    ppermute x6, waiting for transfers between devices, direct(): block = lax.ppermute(block, 'band', perm)  17.3 us
    ppermute x3, waiting for transfers between devices, program_on_device(): lax.ppermute(blocks[k], 'space', shift_perm(n_space, k))  14.7 us
    pallas_call x1, Pallas kernels, inner(): pl.pallas_call(lambda *refs: inner_kernel(n_band, start, *refs), out_shap...  14.3 us
    ppermute x6, waiting for transfers between devices, halving(): got = lax.ppermute(send, 'band', perm)  13.7 us
    ppermute x6, waiting for transfers between devices, to_columns(): lax.ppermute(blocks[k], 'space', shift_perm(n_space, k))  8.61 us
  transfers between devices with their start and end apart: 34, of which 15 were waited for; matrix products, arithmetic and copies ran while one was open for 3% of the time, Pallas kernels for 30%

commit v1 on v0

--- a/solution.py
+++ b/solution.py
@@ -14,6 +14,7 @@
 COEFFS = (-205.0 / 72.0, 8.0 / 5.0, -1.0 / 5.0, 8.0 / 315.0, -1.0 / 560.0)
 DENOM = 5040.0
 MIB = 1 << 20
+MOST = 119 * MIB // 2
 UNROLL = 4
 F32 = jnp.float32
 BF16 = jnp.bfloat16
@@ -548,7 +549,7 @@
             pltpu.VMEM((2, REACH, n, n), BF16), pltpu.VMEM((2, REACH, n, n), F32),
             pltpu.VMEM((whole, LANES), F32), dma((2, 2)),
         ],
-        name="edges", compiler_params=pltpu.CompilerParams(vmem_limit_bytes=12 * MIB),
+        name="edges", compiler_params=pltpu.CompilerParams(vmem_limit_bytes=MOST),
     )(share, orb, pert)
     cores = [(b, b ^ 1) for b in range(n_band)]
     halos = []
@@ -581,7 +582,7 @@
             pltpu.VMEM((count_x, n, n), F32), pltpu.VMEM((count_x, n, n), F32), *stages(),
             dma((3, count_x // REACH)), dma((count_x // REACH,)),
         ],
-        name="first_a", compiler_params=pltpu.CompilerParams(vmem_limit_bytes=52 * MIB),
+        name="first_a", compiler_params=pltpu.CompilerParams(vmem_limit_bytes=MOST),
     )(share, co, orb, pert, pot, *tables)
 
     def inner(start, count):
@@ -594,7 +595,7 @@
                 pltpu.VMEM((count, n, n), BF16), pltpu.VMEM((count, n, n), F32), pltpu.VMEM((count, n, n), F32),
                 pltpu.VMEM((count + 2 * REACH, n, n), F32), *stages(), dma((4, count // 2)), dma((1,)),
             ],
-            compiler_params=pltpu.CompilerParams(vmem_limit_bytes=28 * MIB),
+            compiler_params=pltpu.CompilerParams(vmem_limit_bytes=50 * MIB),
         )(share, co, orb, pert, pot, d1, *tables)
 
     span = 3 * REACH
@@ -610,7 +611,7 @@
                 pltpu.VMEM((span, n, n), F32), pltpu.VMEM((span, n, n), F32), pltpu.VMEM((5 * REACH, n, n), F32),
                 pltpu.VMEM((whole, LANES), F32), *stages(), dma((4,)),
             ],
-            compiler_params=pltpu.CompilerParams(vmem_limit_bytes=28 * MIB),
+            compiler_params=pltpu.CompilerParams(vmem_limit_bytes=46 * MIB),
         )(share, co, orb, pert, pot, d1, *halo, *tables)
 
     def halving(send, keep):

time: 199 us -> 179 us (0.90)
  local copies, waits for them, and re-layouts: 22.5 us -> 1.52 us
    unnamed x52 -> x30, local copies, waits for them, and re-layouts: 19.8 us -> 0.08 us
    pallas_call x1, Pallas kernels: 14.3 us -> 11.6 us  [inner(): pl.pallas_call(lambda *refs: inner_kernel(n_band, start, *refs), out_shap...]
  transfers between devices with their start and end apart: 34 -> 34, of which waited for: 15 -> 18; matrix products, arithmetic and copies ran while one was open for 3% -> 4% of each run, Pallas kernels for 30% -> 33%
where the time goes in v1:
time: 179 us; the launch traced here: 176 us
  Pallas kernels  68.5 us (38%)
  waiting for transfers between devices  62.9 us (35%)
  starting transfers between devices  36.1 us (20%)
  other arithmetic  4.73 us (3%)
  between operations  1.88 us (1%)
    pallas_call x1, Pallas kernels, program_on_device(): pl.pallas_call(lambda *refs: first_kernel(n_band, *refs), out_shape=[shap...  22.7 us
    pallas_call x2, Pallas kernels, outer(): pl.pallas_call(lambda *refs: boundary_kernel(n_band, side, *refs), out_sh...  21.3 us
    ppermute x6, waiting for transfers between devices, direct(): block = lax.ppermute(block, 'band', perm)  16.3 us
    ppermute x3, waiting for transfers between devices, program_on_device(): lax.ppermute(blocks[k], 'space', shift_perm(n_space, k))  14.7 us
    ppermute x6, waiting for transfers between devices, halving(): got = lax.ppermute(send, 'band', perm)  13.4 us
    pallas_call x1, Pallas kernels, inner(): pl.pallas_call(lambda *refs: inner_kernel(n_band, start, *refs), out_shap...  11.6 us
    ppermute x6, waiting for transfers between devices, to_columns(): lax.ppermute(blocks[k], 'space', shift_perm(n_space, k))  8.68 us
    ppermute x6, starting transfers between devices, direct(): block = lax.ppermute(block, 'band', perm)  8.21 us
  transfers between devices with their start and end apart: 34, of which 18 were waited for; matrix products, arithmetic and copies ran while one was open for 4% of the time, Pallas kernels for 33%

profile of v1, /device:TPU:0, one launch (start us, length us, event | category | flops | bytes accessed | tf_op | source)
XLA Modules:
  0.0 175.6 jit_solution(12057474440553615698)
XLA Ops:
  0.0 3.8 %edges.1 = (f32[1728,128]{1,0:T(8,128)}, f32[1728,128]{1,0:T(8,128)}) custom-call(s32[8,8]{1,0:T(8,128)} %constant.101.clone.refs_0_.share_ref, bf16[48,192,192]{2,1,0:T(8,128)(2,1)} %bitcast.25, f32[48,192,192]{2,1,0:T(8,128)} %bitcast.20), custom_call_target="tpu_custom_call" | custom-call | tf_op jit(solution)/shard_map/edges/pallas_call | solution.py:543
  3.8 3.1 %collective-permute-start.11 = (f32[1728,128]{1,0:T(8,128)}, f32[1728,128]{1,0:T(8,128)S(1)}, u32[]{:S(2)}, u32[]{:S(2)}) collective-permute-start(f32[1728,128]{1,0:T(8,128)} %get-tuple-element.45), channel_id=1, source_target_pairs={{0,1},{1,2},{2,3},{3,0},{4,5},{5,6},{6,7},{7,4},{8,9},{9,10},{10,1... | collective-permute-start | bytes 2654216 | tf_op jit(solution)/shard_map/ppermute | solution.py:557
  11.3 22.7 %first_a.1 = (f32[48,192,192]{2,1,0:T(8,128)}, f32[8,3,96,128]{3,2,1,0:T(8,128)}, f32[8,3,96,128]{3,2,1,0:T(8,128)}) custom-call(s32[8,8]{1,0:T(8,128)} %constant.101.clone.refs_0_.share_ref, f32[16]{0:T(128)} %stack.35.refs_1_, bf16[48,192,192]{2,1,0:T(8,128)(2,1)} %bitcast.26, f32[48,192,192]{2,1,0:T(8,128)} %bitcast.21, f32[48,192,192]{2,1,0:T(8,128)} %refs_4_.7, ...), custom_call_target="tpu_custom_call" | custom-call | tf_op jit(solution)/shard_map/first_a/pallas_call | solution.py:575
  34.2 11.6 %shard_map.154 = (f32[8,3,96,128]{3,2,1,0:T(8,128)}, f32[8,3,96,128]{3,2,1,0:T(8,128)S(1)}) custom-call(s32[8,8]{1,0:T(8,128)S(1)} %copy-done.6, f32[16]{0:T(128)S(1)} %copy-done.13, bf16[48,192,192]{2,1,0:T(8,128)(2,1)} %bitcast.27, f32[48,192,192]{2,1,0:T(8,128)} %bitcast.22, f32[48,192,192]{2,1,0:T(8,128)} %refs_4_.7, ...), custom_call_target="tpu_custom_call" | custom-call | tf_op jit(solution)/shard_map/pallas_call | solution.py:589
  49.4 10.9 %shard_map.156 = (f32[6,3,96,128]{3,2,1,0:T(8,128)}, f32[6,3,96,128]{3,2,1,0:T(8,128)S(1)}) custom-call(s32[8,8]{1,0:T(8,128)S(1)} %copy-done.6, f32[16]{0:T(128)S(1)} %copy-done.13, bf16[48,192,192]{2,1,0:T(8,128)(2,1)} %bitcast.28, f32[48,192,192]{2,1,0:T(8,128)} %bitcast.23, f32[48,192,192]{2,1,0:T(8,128)} %refs_4_.7, ...), custom_call_target="tpu_custom_call" | custom-call | tf_op jit(solution)/shard_map/pallas_call | solution.py:604
  60.7 10.4 %shard_map.157 = (f32[6,3,96,128]{3,2,1,0:T(8,128)S(1)}, f32[6,3,96,128]{3,2,1,0:T(8,128)S(1)}) custom-call(s32[8,8]{1,0:T(8,128)S(1)} %copy-done.6, f32[16]{0:T(128)S(1)} %copy-done.13, bf16[48,192,192]{2,1,0:T(8,128)(2,1)} %bitcast.29, f32[48,192,192]{2,1,0:T(8,128)} %bitcast.24, f32[48,192,192]{2,1,0:T(8,128)} %refs_4_.7, ...), custom_call_target="tpu_custom_call" | custom-call | tf_op jit(solution)/shard_map/pallas_call | solution.py:604
  72.9 2.7 %collective-permute-start.1 = (f32[8,3,24,128]{3,2,1,0:T(8,128)S(1)}, f32[8,3,24,128]{3,2,1,0:T(8,128)S(1)}, u32[]{:S(2)}, u32[]{:S(2)}) collective-permute-start(f32[8,3,24,128]{3,2,1,0:T(8,128)S(1)} %get-tuple-element.74), channel_id=1, source_target_pairs={{0,24},{4,28},{8,16},{12,20},{16,8},{20,12},{24,0},{28,4},{1,25},{... | collective-permute-start | bytes 884744 | tf_op jit(solution)/shard_map/ppermute | solution.py:635
  77.9 2.7 %collective-permute-start.5 = (f32[8,3,24,128]{3,2,1,0:T(8,128)S(1)}, f32[8,3,24,128]{3,2,1,0:T(8,128)S(1)}, u32[]{:S(2)}, u32[]{:S(2)}) collective-permute-start(f32[8,3,24,128]{3,2,1,0:T(8,128)S(1)} %get-tuple-element.70), channel_id=1, source_target_pairs={{0,24},{4,28},{8,16},{12,20},{16,8},{20,12},{24,0},{28,4},{1,25},{... | collective-permute-start | bytes 884744 | tf_op jit(solution)/shard_map/ppermute | solution.py:635
  85.4 4.9 %collective-permute-done.2.refs_2_ = f32[8,3,24,128]{3,2,1,0:T(8,128)S(1)} collective-permute-done((f32[8,3,24,128]{3,2,1,0:T(8,128)S(1)}, f32[8,3,24,128]{3,2,1,0:T(8,128)S(1)}, u32[]{:S(2)}, u32[]{:S(2)}) %collective-permute-start.2) | collective-permute-done | bytes 294944 | tf_op jit(solution)/shard_map/ppermute | solution.py:635
  92.9 3.6 %collective-permute-done.5.refs_5_ = f32[8,3,24,128]{3,2,1,0:T(8,128)S(1)} collective-permute-done((f32[8,3,24,128]{3,2,1,0:T(8,128)S(1)}, f32[8,3,24,128]{3,2,1,0:T(8,128)S(1)}, u32[]{:S(2)}, u32[]{:S(2)}) %collective-permute-start.5) | collective-permute-done | bytes 294944 | tf_op jit(solution)/shard_map/ppermute | solution.py:635
  96.5 5.9 %collective-permute-done.6.refs_6_ = f32[8,3,24,128]{3,2,1,0:T(8,128)S(1)} collective-permute-done((f32[8,3,24,128]{3,2,1,0:T(8,128)S(1)}, f32[8,3,24,128]{3,2,1,0:T(8,128)S(1)}, u32[]{:S(2)}, u32[]{:S(2)}) %collective-permute-start.6) | collective-permute-done | bytes 294944 | tf_op jit(solution)/shard_map/ppermute | solution.py:635
  103.9 3.2 %collective-permute-done.14 = f32[6,3,48,128]{3,2,1,0:T(8,128)S(1)} collective-permute-done((f32[6,3,48,128]{3,2,1,0:T(8,128)S(1)}, f32[6,3,48,128]{3,2,1,0:T(8,128)S(1)}, u32[]{:S(2)}, u32[]{:S(2)}) %collective-permute-start.14) | collective-permute-done | bytes 442400 | tf_op jit(solution)/shard_map/ppermute | solution.py:620
  107.6 6.5 %collective-permute-done.19 = f32[6,3,48,128]{3,2,1,0:T(8,128)S(1)} collective-permute-done((f32[6,3,48,128]{3,2,1,0:T(8,128)S(1)}, f32[6,3,48,128]{3,2,1,0:T(8,128)S(1)}, u32[]{:S(2)}, u32[]{:S(2)}) %collective-permute-start.19) | collective-permute-done | bytes 442400 | tf_op jit(solution)/shard_map/ppermute | solution.py:620
  116.5 3.7 %collective-permute-done.20.refs_4_ = f32[6,3,24,128]{3,2,1,0:T(8,128)S(1)} collective-permute-done((f32[6,3,24,128]{3,2,1,0:T(8,128)S(1)}, f32[6,3,24,128]{3,2,1,0:T(8,128)S(1)}, u32[]{:S(2)}, u32[]{:S(2)}) %collective-permute-start.20) | collective-permute-done | bytes 221216 | tf_op jit(solution)/shard_map/ppermute | solution.py:620
  125.1 3.2 %collective-permute-done.21.refs_6_ = f32[9,24,128]{2,1,0:T(8,128)S(1)} collective-permute-done((f32[9,24,128]{2,1,0:T(8,128)S(1)}, f32[9,24,128]{2,1,0:T(8,128)S(1)}, u32[]{:S(2)}, u32[]{:S(2)}) %collective-permute-start.21) | collective-permute-done | bytes 110624 | tf_op jit(solution)/shard_map/ppermute | solution.py:651
  128.3 5.4 %collective-permute-done.22.refs_7_ = f32[9,24,128]{2,1,0:T(8,128)S(1)} collective-permute-done((f32[9,24,128]{2,1,0:T(8,128)S(1)}, f32[9,24,128]{2,1,0:T(8,128)S(1)}, u32[]{:S(2)}, u32[]{:S(2)}) %collective-permute-start.22) | collective-permute-done | bytes 110624 | tf_op jit(solution)/shard_map/ppermute | solution.py:651
  136.0 2.9 %collective-permute-start.24 = (f32[9,48,128]{2,1,0:T(8,128)S(1)}, f32[9,48,128]{2,1,0:T(8,128)S(1)}, u32[]{:S(2)}, u32[]{:S(2)}) collective-permute-start(f32[9,48,128]{2,1,0:T(8,128)S(1)} %get-tuple-element.56), channel_id=1, source_target_pairs={{0,1},{1,2},{2,3},{3,0},{4,5},{5,6},{6,7},{7,4},{8,9},{9,10},{10,1... | collective-permute-start | bytes 663560 | tf_op jit(solution)/shard_map/ppermute | solution.py:716
  138.8 2.5 %collective-permute-start.25 = (f32[9,48,128]{2,1,0:T(8,128)S(1)}, f32[9,48,128]{2,1,0:T(8,128)S(1)}, u32[]{:S(2)}, u32[]{:S(2)}) collective-permute-start(f32[9,48,128]{2,1,0:T(8,128)S(1)} %get-tuple-element.57), channel_id=1, source_target_pairs={{0,2},{1,3},{2,0},{3,1},{4,6},{5,7},{6,4},{7,5},{8,10},{9,11},{10,... | collective-permute-start | bytes 663560 | tf_op jit(solution)/shard_map/ppermute | solution.py:716
  141.3 5.9 %collective-permute-done.24.refs_2_ = f32[9,48,128]{2,1,0:T(8,128)S(1)} collective-permute-done((f32[9,48,128]{2,1,0:T(8,128)S(1)}, f32[9,48,128]{2,1,0:T(8,128)S(1)}, u32[]{:S(2)}, u32[]{:S(2)}) %collective-permute-start.24) | collective-permute-done | bytes 221216 | tf_op jit(solution)/shard_map/ppermute | solution.py:716
  147.2 8.8 %collective-permute-done.25.refs_3_ = f32[9,48,128]{2,1,0:T(8,128)S(1)} collective-permute-done((f32[9,48,128]{2,1,0:T(8,128)S(1)}, f32[9,48,128]{2,1,0:T(8,128)S(1)}, u32[]{:S(2)}, u32[]{:S(2)}) %collective-permute-start.25) | collective-permute-done | bytes 221216 | tf_op jit(solution)/shard_map/ppermute | solution.py:716
  156.0 2.3 %shard_map.159 = (f32[240,128]{1,0:T(8,128)S(1)}, f32[240,128]{1,0:T(8,128)S(1)}, f32[240,128]{1,0:T(8,128)S(1)}, f32[240,128]{1,0:T(8,128)S(1)}, f32[240,128]{1...) custom-call(s32[8,8]{1,0:T(8,128)S(1)} %copy-done.6, ...), custom_call_target="tpu_custom_call" | custom-call | tf_op jit(solution)/shard_map/pallas_call | solution.py:717
  162.0 2.5 %collective-permute-start.32 = (f32[240,128]{1,0:T(8,128)S(1)}, f32[240,128]{1,0:T(8,128)S(1)}, u32[]{:S(2)}, u32[]{:S(2)}) collective-permute-start(f32[240,128]{1,0:T(8,128)S(1)} %get-tuple-element.65), channel_id=1, source_target_pairs={{0,24},{4,28},{8,16},{12,20},{16,8},{20,12},{24,0},{28,4},{1,25},{... | collective-permute-start | bytes 368648 | tf_op jit(solution)/shard_map/ppermute | solution.py:731
  166.5 6.7 %collective-permute-done.31.refs_6_ = f32[240,128]{1,0:T(8,128)S(1)} collective-permute-done((f32[240,128]{1,0:T(8,128)S(1)}, f32[240,128]{1,0:T(8,128)S(1)}, u32[]{:S(2)}, u32[]{:S(2)}) %collective-permute-start.31) | collective-permute-done | bytes 122912 | tf_op jit(solution)/shard_map/ppermute | solution.py:731
  173.2 2.5 %along_z.1 = f32[48,24,192]{2,1,0:T(8,128)} custom-call(s32[8,8]{1,0:T(8,128)S(1)} %copy-done.6, f32[240,128]{1,0:T(8,128)S(1)} %get-tuple-element.59.refs_1_, f32[240,128]{1,0:T(8,128)S(1)} %collective-permute-done.27.refs_2_, f32[240,128]{1,0:T(8,128)S(1)} %collective-permute-done.28.refs_3_, f32[240,128]{1,0:T(8,128)S(1)} %collective-permute-done.29.refs_4_, ...), custom_call_target="tpu_custom_call" | custom-call | tf_op jit(solution)/shard_map/along_z/pallas_call | solution.py:736
  (100 shorter events, 35.5 us)
Async XLA Ops:
  3.8 42.4 %collective-permute-start.11 = (f32[1728,128]{1,0:T(8,128)}, f32[1728,128]{1,0:T(8,128)S(1)}, u32[]{:S(2)}, u32[]{:S(2)}) collective-permute-start(f32[1728,128]{1,0:T(8,128)} %get-tuple-element.45), channel_id=1, source_target_pairs={{0,1},{1,2},{2,3},{3,0},{4,5},{5,6},{6,7},{7,4},{8,9},{9,10},{10,1... | collective-permute-start | bytes 2654216 | tf_op jit(solution)/shard_map/ppermute | solution.py:557
  6.9 40.3 %collective-permute-start.16 = (f32[1728,128]{1,0:T(8,128)}, f32[1728,128]{1,0:T(8,128)S(1)}, u32[]{:S(2)}, u32[]{:S(2)}) collective-permute-start(f32[1728,128]{1,0:T(8,128)} %get-tuple-element.48), channel_id=1, source_target_pairs={{0,3},{1,0},{2,1},{3,2},{4,7},{5,4},{6,5},{7,6},{8,11},{9,8},{10,9... | collective-permute-start | bytes 2654216 | tf_op jit(solution)/shard_map/ppermute | solution.py:557
  34.0 37.4 %collective-permute-start = (f32[8,3,96,128]{3,2,1,0:T(8,128)}, f32[8,3,96,128]{3,2,1,0:T(8,128)}, u32[]{:S(2)}, u32[]{:S(2)}) collective-permute-start(f32[8,3,96,128]{3,2,1,0:T(8,128)} %get-tuple-element.37), channel_id=1, source_target_pairs={{0,4},{4,0},{8,12},{12,8},{16,20},{20,16},{24,28},{28,24},{1,5},{5... | collective-permute-start | bytes 3538952 | tf_op jit(solution)/shard_map/ppermute | solution.py:628
  45.7 30.4 %collective-permute-start.4 = (f32[8,3,96,128]{3,2,1,0:T(8,128)}, f32[8,3,96,128]{3,2,1,0:T(8,128)}, u32[]{:S(2)}, u32[]{:S(2)}) collective-permute-start(f32[8,3,96,128]{3,2,1,0:T(8,128)} %get-tuple-element.40), channel_id=1, source_target_pairs={{0,4},{4,0},{8,12},{12,8},{16,20},{20,16},{24,28},{28,24},{1,5},{5... | collective-permute-start | bytes 3538952 | tf_op jit(solution)/shard_map/ppermute | solution.py:628
  47.9 12.8 %collective-permute-start.17 = (f32[576,128]{1,0:T(8,128)}, f32[576,128]{1,0:T(8,128)}, u32[]{:S(2)}, u32[]{:S(2)}) collective-permute-start(f32[576,128]{1,0:T(8,128)} %slice.151), channel_id=1, source_target_pairs={{0,4},{4,0},{8,12},{12,8},{16,20},{20,16},{24,28},{28,24},{1,5},{5... | collective-permute-start | bytes 884744 | tf_op jit(solution)/shard_map/ppermute | solution.py:558
  60.3 17.6 %collective-permute-start.13 = (f32[6,3,96,128]{3,2,1,0:T(8,128)}, f32[6,3,96,128]{3,2,1,0:T(8,128)}, u32[]{:S(2)}, u32[]{:S(2)}) collective-permute-start(f32[6,3,96,128]{3,2,1,0:T(8,128)} %get-tuple-element.47), channel_id=1, source_target_pairs={{0,4},{4,0},{8,12},{12,8},{16,20},{20,16},{24,28},{28,24},{1,5},{5... | collective-permute-start | bytes 2654216 | tf_op jit(solution)/shard_map/ppermute | solution.py:620
  71.2 19.5 %collective-permute-start.18 = (f32[6,3,96,128]{3,2,1,0:T(8,128)S(1)}, f32[6,3,96,128]{3,2,1,0:T(8,128)S(1)}, u32[]{:S(2)}, u32[]{:S(2)}) collective-permute-start(f32[6,3,96,128]{3,2,1,0:T(8,128)S(1)} %get-tuple-element.50), channel_id=1, source_target_pairs={{0,4},{4,0},{8,12},{12,8},{16,20},{20,16},{24,28},{28,24},{1,5},{5... | collective-permute-start | bytes 2654216 | tf_op jit(solution)/shard_map/ppermute | solution.py:620
  72.9 10.9 %collective-permute-start.1 = (f32[8,3,24,128]{3,2,1,0:T(8,128)S(1)}, f32[8,3,24,128]{3,2,1,0:T(8,128)S(1)}, u32[]{:S(2)}, u32[]{:S(2)}) collective-permute-start(f32[8,3,24,128]{3,2,1,0:T(8,128)S(1)} %get-tuple-element.74), channel_id=1, source_target_pairs={{0,24},{4,28},{8,16},{12,20},{16,8},{20,12},{24,0},{28,4},{1,25},{... | collective-permute-start | bytes 884744 | tf_op jit(solution)/shard_map/ppermute | solution.py:635
  75.6 14.8 %collective-permute-start.2 = (f32[8,3,24,128]{3,2,1,0:T(8,128)S(1)}, f32[8,3,24,128]{3,2,1,0:T(8,128)S(1)}, u32[]{:S(2)}, u32[]{:S(2)}) collective-permute-start(f32[8,3,24,128]{3,2,1,0:T(8,128)S(1)} %get-tuple-element.73), channel_id=1, source_target_pairs={{0,8},{4,20},{8,0},{12,28},{16,24},{20,4},{24,16},{28,12},{1,9},{5... | collective-permute-start | bytes 884744 | tf_op jit(solution)/shard_map/ppermute | solution.py:635
  76.1 16.3 %collective-permute-start.3 = (f32[8,3,24,128]{3,2,1,0:T(8,128)S(1)}, f32[8,3,24,128]{3,2,1,0:T(8,128)S(1)}, u32[]{:S(2)}, u32[]{:S(2)}) collective-permute-start(f32[8,3,24,128]{3,2,1,0:T(8,128)S(1)} %get-tuple-element.72), channel_id=1, source_target_pairs={{0,16},{4,12},{8,24},{12,4},{16,0},{20,28},{24,8},{28,20},{1,17},{... | collective-permute-start | bytes 884744 | tf_op jit(solution)/shard_map/ppermute | solution.py:635
  77.9 18.6 %collective-permute-start.5 = (f32[8,3,24,128]{3,2,1,0:T(8,128)S(1)}, f32[8,3,24,128]{3,2,1,0:T(8,128)S(1)}, u32[]{:S(2)}, u32[]{:S(2)}) collective-permute-start(f32[8,3,24,128]{3,2,1,0:T(8,128)S(1)} %get-tuple-element.70), channel_id=1, source_target_pairs={{0,24},{4,28},{8,16},{12,20},{16,8},{20,12},{24,0},{28,4},{1,25},{... | collective-permute-start | bytes 884744 | tf_op jit(solution)/shard_map/ppermute | solution.py:635
  83.8 18.6 %collective-permute-start.6 = (f32[8,3,24,128]{3,2,1,0:T(8,128)S(1)}, f32[8,3,24,128]{3,2,1,0:T(8,128)S(1)}, u32[]{:S(2)}, u32[]{:S(2)}) collective-permute-start(f32[8,3,24,128]{3,2,1,0:T(8,128)S(1)} %get-tuple-element.69), channel_id=1, source_target_pairs={{0,8},{4,20},{8,0},{12,28},{16,24},{20,4},{24,16},{28,12},{1,9},{5... | collective-permute-start | bytes 884744 | tf_op jit(solution)/shard_map/ppermute | solution.py:635
  90.3 12.1 %collective-permute-start.7 = (f32[8,3,24,128]{3,2,1,0:T(8,128)S(1)}, f32[8,3,24,128]{3,2,1,0:T(8,128)S(1)}, u32[]{:S(2)}, u32[]{:S(2)}) collective-permute-start(f32[8,3,24,128]{3,2,1,0:T(8,128)S(1)} %get-tuple-element.68), channel_id=1, source_target_pairs={{0,16},{4,12},{8,24},{12,4},{16,0},{20,28},{24,8},{28,20},{1,17},{... | collective-permute-start | bytes 884744 | tf_op jit(solution)/shard_map/ppermute | solution.py:635
  90.7 16.5 %collective-permute-start.14 = (f32[6,3,48,128]{3,2,1,0:T(8,128)S(1)}, f32[6,3,48,128]{3,2,1,0:T(8,128)S(1)}, u32[]{:S(2)}, u32[]{:S(2)}) collective-permute-start(f32[6,3,48,128]{3,2,1,0:T(8,128)S(1)} %get-tuple-element.78), channel_id=1, source_target_pairs={{0,8},{4,20},{8,0},{12,28},{16,24},{20,4},{24,16},{28,12},{1,9},{5... | collective-permute-start | bytes 1327112 | tf_op jit(solution)/shard_map/ppermute | solution.py:620
  92.4 21.6 %collective-permute-start.19 = (f32[6,3,48,128]{3,2,1,0:T(8,128)S(1)}, f32[6,3,48,128]{3,2,1,0:T(8,128)S(1)}, u32[]{:S(2)}, u32[]{:S(2)}) collective-permute-start(f32[6,3,48,128]{3,2,1,0:T(8,128)S(1)} %get-tuple-element.76), channel_id=1, source_target_pairs={{0,8},{4,20},{8,0},{12,28},{16,24},{20,4},{24,16},{28,12},{1,9},{5... | collective-permute-start | bytes 1327112 | tf_op jit(solution)/shard_map/ppermute | solution.py:620
  103.7 19.5 %collective-permute-start.8 = (f32[9,32,128]{2,1,0:T(8,128)S(1)}, f32[9,32,128]{2,1,0:T(8,128)S(1)}, u32[]{:S(2)}, u32[]{:S(2)}) collective-permute-start(f32[9,32,128]{2,1,0:T(8,128)S(1)} %get-tuple-element.42), channel_id=1, source_target_pairs={{0,1},{1,2},{2,3},{3,0},{4,5},{5,6},{6,7},{7,4},{8,9},{9,10},{10,1... | collective-permute-start | bytes 442376 | tf_op jit(solution)/shard_map/ppermute | solution.py:651
  114.4 10.7 %collective-permute-start.9 = (f32[9,32,128]{2,1,0:T(8,128)S(1)}, f32[9,32,128]{2,1,0:T(8,128)S(1)}, u32[]{:S(2)}, u32[]{:S(2)}) collective-permute-start(f32[9,32,128]{2,1,0:T(8,128)S(1)} %get-tuple-element.43), channel_id=1, source_target_pairs={{0,2},{1,3},{2,0},{3,1},{4,6},{5,7},{6,4},{7,5},{8,10},{9,11},{10,... | collective-permute-start | bytes 442376 | tf_op jit(solution)/shard_map/ppermute | solution.py:651
  121.0 12.7 %collective-permute-start.22 = (f32[9,24,128]{2,1,0:T(8,128)S(1)}, f32[9,24,128]{2,1,0:T(8,128)S(1)}, u32[]{:S(2)}, u32[]{:S(2)}) collective-permute-start(f32[9,24,128]{2,1,0:T(8,128)S(1)} %get-tuple-element.53), channel_id=1, source_target_pairs={{0,2},{1,3},{2,0},{3,1},{4,6},{5,7},{6,4},{7,5},{8,10},{9,11},{10,... | collective-permute-start | bytes 331784 | tf_op jit(solution)/shard_map/ppermute | solution.py:651
  123.2 10.5 %collective-permute-start.23 = (f32[9,24,128]{2,1,0:T(8,128)S(1)}, f32[9,24,128]{2,1,0:T(8,128)S(1)}, u32[]{:S(2)}, u32[]{:S(2)}) collective-permute-start(f32[9,24,128]{2,1,0:T(8,128)S(1)} %get-tuple-element.54), channel_id=1, source_target_pairs={{0,3},{1,0},{2,1},{3,2},{4,7},{5,4},{6,5},{7,6},{8,11},{9,8},{10,9... | collective-permute-start | bytes 331784 | tf_op jit(solution)/shard_map/ppermute | solution.py:651
  136.0 11.2 %collective-permute-start.24 = (f32[9,48,128]{2,1,0:T(8,128)S(1)}, f32[9,48,128]{2,1,0:T(8,128)S(1)}, u32[]{:S(2)}, u32[]{:S(2)}) collective-permute-start(f32[9,48,128]{2,1,0:T(8,128)S(1)} %get-tuple-element.56), channel_id=1, source_target_pairs={{0,1},{1,2},{2,3},{3,0},{4,5},{5,6},{6,7},{7,4},{8,9},{9,10},{10,1... | collective-permute-start | bytes 663560 | tf_op jit(solution)/shard_map/ppermute | solution.py:716
  138.8 17.2 %collective-permute-start.25 = (f32[9,48,128]{2,1,0:T(8,128)S(1)}, f32[9,48,128]{2,1,0:T(8,128)S(1)}, u32[]{:S(2)}, u32[]{:S(2)}) collective-permute-start(f32[9,48,128]{2,1,0:T(8,128)S(1)} %get-tuple-element.57), channel_id=1, source_target_pairs={{0,2},{1,3},{2,0},{3,1},{4,6},{5,7},{6,4},{7,5},{8,10},{9,11},{10,... | collective-permute-start | bytes 663560 | tf_op jit(solution)/shard_map/ppermute | solution.py:716
  141.3 14.7 %collective-permute-start.26 = (f32[9,48,128]{2,1,0:T(8,128)S(1)}, f32[9,48,128]{2,1,0:T(8,128)S(1)}, u32[]{:S(2)}, u32[]{:S(2)}) collective-permute-start(f32[9,48,128]{2,1,0:T(8,128)S(1)} %get-tuple-element.58), channel_id=1, source_target_pairs={{0,3},{1,0},{2,1},{3,2},{4,7},{5,4},{6,5},{7,6},{8,11},{9,8},{10,9... | collective-permute-start | bytes 663560 | tf_op jit(solution)/shard_map/ppermute | solution.py:716
  161.6 11.5 %collective-permute-start.31 = (f32[240,128]{1,0:T(8,128)S(1)}, f32[240,128]{1,0:T(8,128)S(1)}, u32[]{:S(2)}, u32[]{:S(2)}) collective-permute-start(f32[240,128]{1,0:T(8,128)S(1)} %get-tuple-element.64), channel_id=1, source_target_pairs={{0,20},{4,16},{8,28},{12,24},{16,4},{20,0},{24,12},{28,8},{1,21},{... | collective-permute-start | bytes 368648 | tf_op jit(solution)/shard_map/ppermute | solution.py:731
  162.0 11.2 %collective-permute-start.32 = (f32[240,128]{1,0:T(8,128)S(1)}, f32[240,128]{1,0:T(8,128)S(1)}, u32[]{:S(2)}, u32[]{:S(2)}) collective-permute-start(f32[240,128]{1,0:T(8,128)S(1)} %get-tuple-element.65), channel_id=1, source_target_pairs={{0,24},{4,28},{8,16},{12,20},{16,8},{20,12},{24,0},{28,4},{1,25},{... | collective-permute-start | bytes 368648 | tf_op jit(solution)/shard_map/ppermute | solution.py:731
  (25 other events, 375.3 us)
